TPU v7x, 256 devices: a whole 4x4x8 slice. The times are simulated.
256 devices in a mesh: row: 32 (over z_hi, y, core), col: 8 (over z_lo, x).
Axes of the slice: x: 4, y: 4, z: 8 (z_hi: 4, z_lo: 2; z = z_hi * 2 + z_lo), core: 2. Of those that a mesh axis runs over, the one named last changes fastest.
Arguments:
- left: float32 [128, 16384], P('col', 'row'), may hold values from -12 to 12
- right: float32 [128, 16384], P('row', 'col'), may hold values from -12 to 12
- w_out: float32 [1024, 128], replicated, may hold values from -0.1875 to 0.1875
- b_out: float32 [128], replicated, may hold values from -3 to 3
- pair_grad: float32 [512, 512, 128], P('row', 'col'), may hold values from -6 to 6
Outputs:
- pair_out: float32 [512, 512, 128], P('row', 'col')
- grad_left: float32 [128, 16384], P('col', 'row')
- grad_right: float32 [128, 16384], P('row', 'col')
- grad_weight: float32 [1024, 128], replicated
- grad_bias: float32 [128], replicated
All inputs are finite; a program needn't handle non-finite values.
Results may differ from a plain program's by a relative error of at most 0.0001.
Values sent between devices are 32-bit elements; how exact they have to be, the bound alone decides.
No kernel may reach another device: no remote copies, remote signals or barrier semaphores. Data moves between devices by JAX's collectives and lax.ppermute only.
A program may use at most 128 MiB of HBM per device.

v0:
```python
import jax
import jax.numpy as jnp
from jax import lax
from jax.sharding import PartitionSpec as P

C = 32
Z = 128
S = 128


def body(left, right, w_out, b_out, pair_grad):
    highest = lax.Precision.HIGHEST
    tile_rows = left.shape[1] // C
    tile_cols = right.shape[1] // C
    residues = tile_rows * lax.axis_size("row")
    weight_cube = w_out.reshape(C, C, Z)
    contract_rows = (((0,), (0,)), ((), ()))
    contract_cols = (((1,), (1,)), ((), ()))
    left_all = lax.all_gather(left, "col", axis=0, tiled=True)
    right_all = lax.all_gather(right, "row", axis=0, tiled=True)
    outer = (
        lax.dot_general(
            left_all,
            right_all,
            contract_rows,
            precision=highest,
            preferred_element_type=jnp.float32,
        )
        / S
    )
    outer_split = outer.reshape(tile_rows, C, tile_cols, C)
    pair_out = jnp.einsum("icje,cez->ijz", outer_split, weight_cube, precision=highest) + b_out
    grad_outer = jnp.einsum("ijz,cez->icje", pair_grad, weight_cube, precision=highest)
    grad_outer = grad_outer.reshape(tile_rows * C, tile_cols * C)
    grad_left = lax.psum_scatter(
        lax.dot_general(
            right_all,
            grad_outer,
            contract_cols,
            precision=highest,
            preferred_element_type=jnp.float32,
        )
        / S,
        "col",
        scatter_dimension=0,
        tiled=True,
    )
    grad_right = lax.psum_scatter(
        jnp.dot(left_all, grad_outer, precision=highest) / S, "row", scatter_dimension=0, tiled=True
    )
    weight_term = jnp.einsum("icje,ijz->cez", outer_split, pair_grad, precision=highest).reshape(
        C * C, Z
    )
    bias_term = jnp.sum(pair_grad, axis=(0, 1))
    grad_weight, grad_bias = lax.psum((weight_term, bias_term), ("row", "col"))
    return (pair_out, grad_left, grad_right, grad_weight / residues, grad_bias / residues)


def solution(mesh):
    placed = (P("col", "row"), P("row", "col"), P(), P(), P("row", "col", None))
    return jax.shard_map(
        body,
        mesh=mesh,
        in_specs=placed,
        out_specs=(P("row", "col", None), P("col", "row"), P("row", "col"), P(), P()),
        check_vma=False,
    )
```

profile of v0, /device:TPU:8, one launch (start us, length us, event | category | flops | bytes accessed | tf_op | source)
XLA Modules:
  0.0 770.1 jit_solution(7213743941106208333)
XLA Ops:
  7.2 0.0 copy-start
  7.2 0.0 all-reduce.6.cloned.1.call-start
  7.2 29.5 %all_gather.6 = f32[128,512]{1,0:T(8,128)S(1)} all-gather(f32[16,512]{1,0:T(8,128)} %param.5), channel_id=1, replica_groups=mesh['row'=32,'col'=8] {'col'}, dimensions={0}, use_global_device_ids=true | all-gather | bytes 294912 | tf_op jit(solution)/shard_map/all_gather | solution.py:19
  36.8 0.0 copy-done
  36.8 9.8 %convolution_bitcast_fusion = f32[16,32,64,32]{2,3,0,1:T(8,128)} fusion(f32[32,32,128,1]{2,1,3,0:T(8,128)S(1)} %bitcast.42, f32[16,64,128]{2,1,0:T(8,128)} %param.9), kind=kOutput, calls=%fused_computation.1 | convolution fusion | flops 1610612736 | bytes 5242880 | tf_op jit(solution)/shard_map/ijz,cez->icje/dot_general | solution.py:33
  46.6 12.3 %copy.21 = f32[16,32,64,32]{3,2,1,0:T(8,128)} copy(f32[16,32,64,32]{2,3,0,1:T(8,128)} %convolution_bitcast_fusion) | data formatting | bytes 8388608 | tf_op jit(solution)/shard_map/ijz,cez->icje/transpose | solution.py:33
  58.9 0.0 copy-start.1
  58.9 0.0 copy-start.3
  58.9 13.5 %reshape.24 = f32[512,2048]{1,0:T(8,128)} reshape(f32[16,32,64,32]{3,2,1,0:T(8,128)} %copy.21) | data formatting | bytes 8388608 | tf_op jit(solution)/shard_map/reshape | solution.py:34
  72.4 9.9 %fusion = f32[128,2048]{0,1:T(8,128)} fusion(f32[512,2048]{1,0:T(8,128)} %reshape.24, f32[128,512]{1,0:T(8,128)S(1)} %all_gather.6), kind=kOutput, calls=%fused_computation.3 | convolution fusion | flops 1610874880 | bytes 5505024 | tf_op jit(solution)/shard_map/dot_general | solution.py:49
  82.2 0.0 all-reduce.6.cloned.1.call-update
  82.3 0.0 all-gather.3.cloned.1.call-start
  82.3 0.7 all-gather.3.cloned.1.call-update
  83.0 0.2 all-reduce.4.cloned.1.call-start
  83.2 0.0 copy-done.1
  83.3 0.2 reduce_sum.9
  83.4 0.0 copy-done.3
  83.4 0.6 dynamic-slice
  84.7 77.5 %psum.15 = f32[128]{0:T(128)S(1)} all-reduce(f32[128]{0:T(128)S(1)} %reduce_sum.9), channel_id=1, replica_groups=mesh['row'=32,'col'=8] {'row','col'}, use_global_device_ids=true, to_apply=%region_4.0 | all-reduce | flops 128 | bytes 1024 | tf_op jit(solution)/shard_map/psum | solution.py:55
  162.1 0.5 broadcast_multiply_fusion.1
  162.6 205.9 %all-reduce.6.cloned.1.call-done = f32[128,2048]{0,1:T(8,128)} async-done(((f32[128,2048]{0,1:T(8,128)}), f32[128,2048]{0,1:T(8,128)}) %all-reduce.6.cloned.1.call-update) | async-done | bytes 1048592
  368.6 1.6 constant_dynamic-slice_fusion
  370.1 0.9 copy.25
  371.1 55.6 %all-gather.3.cloned.1.call-done = f32[32,4,2048]{2,1,0:T(4,128)} async-done(((f32[1,4,2048]{2,1,0:T(4,128)}), f32[32,4,2048]{2,1,0:T(4,128)}) %all-gather.3.cloned.1.call-update) | async-done | bytes 1048592 | tf_op jit(solution)/shard_map/all_gather | solution.py:20
  426.7 1.6 reshape.26
  428.3 5.0 convolution_multiply_fusion
  433.3 11.4 %reshape.22 = f32[16,32,64,32]{3,2,1,0:T(8,128)} reshape(f32[512,2048]{1,0:T(8,128)} %convolution_multiply_fusion) | data formatting | bytes 8388608 | tf_op jit(solution)/shard_map/reshape | solution.py:31
  444.7 12.7 %copy.33 = f32[32,32,16,64]{3,1,0,2:T(8,128)} copy(f32[32,32,16,64]{1,3,0,2:T(8,128)} %bitcast.44) | data formatting | bytes 8388608 | tf_op jit(solution)/shard_map/icje,ijz->cez/dot_general | solution.py:51
  457.4 0.0 copy-start.2
  457.4 9.9 %convolution_bitcast_fusion.2 = f32[1024,128]{1,0:T(8,128)} fusion(f32[1024,16,64]{2,0,1:T(8,128)} %bitcast.45, f32[16,64,128]{2,1,0:T(8,128)S(1)} %copy-done.1), kind=kOutput, calls=%fused_computation.5 | convolution fusion | flops 1610612736 | bytes 5242880 | tf_op jit(solution)/shard_map/icje,ijz->cez/dot_general | solution.py:51
  467.3 0.0 all-reduce.4.cloned.1.call-update
  467.3 0.3 reduce-scatter.5.cloned.1.call-start
  467.6 5.2 fusion.2
  472.8 0.8 copy.29
  473.7 0.0 reduce-scatter.5.cloned.1.call-update
  473.7 0.0 copy-done.2
  473.7 17.6 %fusion.1 = f32[16,64,128]{2,1,0:T(8,128)} fusion(f32[16,32,64,32]{3,2,1,0:T(8,128)} %reshape.22, f32[32,32,128,1]{2,1,0,3:T(8,128)S(1)} %bitcast.43, f32[128]{0:T(128)S(1)} %copy-done.2), kind=kOutput, calls=%fused_computation.6 | convolution fusion | flops 1610743808 | bytes 5243392 | tf_op jit(solution)/shard_map/icje,cez->ijz/dot_general | solution.py:32
  491.3 230.2 %all-reduce.4.cloned.1.call-done = f32[1024,128]{1,0:T(8,128)} async-done(((f32[1024,128]{1,0:T(8,128)}), f32[1024,128]{1,0:T(8,128)}) %all-reduce.4.cloned.1.call-update) | async-done | bytes 524304 | tf_op jit(solution)/shard_map/psum | solution.py:55
  721.5 1.9 broadcast_multiply_fusion
  723.4 40.2 %reduce-scatter.5.cloned.1.call-done = f32[16,512]{1,0:T(8,128)} async-done(((f32[128,512]{1,0:T(8,128)}), f32[16,512]{1,0:T(8,128)}) %reduce-scatter.5.cloned.1.call-update) | async-done | bytes 32784
Async XLA Ops:
  7.2 29.6 %copy-start = (f32[1024,128]{1,0:T(8,128)S(1)}, f32[1024,128]{1,0:T(8,128)}, u32[]{:S(2)}) copy-start(f32[1024,128]{1,0:T(8,128)} %param.7) | copy-start | bytes 1572868
  7.2 361.4 %all-reduce.6.cloned.1.call-start = ((), (), s32[]{:S(2)}) async-start(), calls=%async_computation.4 | async-start | bytes 2097152
  58.9 24.3 %copy-start.1 = (f32[16,64,128]{2,1,0:T(8,128)S(1)}, f32[16,64,128]{2,1,0:T(8,128)}, u32[]{:S(2)}) copy-start(f32[16,64,128]{2,1,0:T(8,128)} %param.9) | copy-start | bytes 1572868
  58.9 24.5 %copy-start.3 = (u32[256]{0:T(256)S(1)}, u32[256]{0:T(256)}, u32[]{:S(2)}) copy-start(u32[256]{0:T(256)} %constant.18) | copy-start | bytes 3076
  82.3 344.4 %all-gather.3.cloned.1.call-start = ((), (), s32[]{:S(2)}) async-start(), calls=%async_computation.2 | async-start | bytes 1081344 | tf_op jit(solution)/shard_map/all_gather | solution.py:20
  83.0 638.5 %all-reduce.4.cloned.1.call-start = ((), (), s32[]{:S(2)}) async-start(), calls=%async_computation.1 | async-start | bytes 1048576 | tf_op jit(solution)/shard_map/psum | solution.py:55
  457.4 16.3 %copy-start.2 = (f32[128]{0:T(128)S(1)}, f32[128]{0:T(128)}, u32[]{:S(2)}) copy-start(f32[128]{0:T(128)} %param.8) | copy-start | bytes 1540
  467.3 296.3 %reduce-scatter.5.cloned.1.call-start = ((), (), s32[]{:S(2)}) async-start(), calls=%async_computation.3 | async-start | bytes 294912
Sparse Core Ops, SparseCore 0:
  82.4 286.1 all-reduce.5
  371.1 55.5 all-gather.2
  467.4 254.0 all-reduce.3
  724.4 39.1 reduce-scatter.4
where the time goes:
time: 771 us; the launch traced here: 770 us
  waiting for transfers between devices  533 us (69%)
  blocking collectives  107 us (14%)
  matrix products  57.4 us (7%)
  local copies, waits for them, and re-layouts  55.4 us (7%)
  between operations  14.5 us (2%)
    unnamed x6, waiting for transfers between devices  247 us
    psum x1, waiting for transfers between devices, body(): grad_weight, grad_bias = lax.psum((weight_term, bias_term), ('row', 'col'))  230 us
    psum x1, blocking collectives, body(): grad_weight, grad_bias = lax.psum((weight_term, bias_term), ('row', 'col'))  77.5 us
    all_gather x1, waiting for transfers between devices, body(): right_all = lax.all_gather(right, 'row', axis=0, tiled=True)  55.6 us
    all_gather x1, blocking collectives, body(): left_all = lax.all_gather(left, 'col', axis=0, tiled=True)  29.5 us
    dot_general x1, matrix products, body(): jnp.einsum('icje,cez->ijz', outer_split, weight_cube, precision=highest)  17.6 us
  transfers between devices with their start and end apart: 4, of which 4 were waited for; matrix products, arithmetic and copies ran while one was open for 4% of the time, Pallas kernels for 0%

commit v1 on v0

--- a/solution.py
+++ b/solution.py
@@ -52,7 +52,7 @@
         C * C, Z
     )
     bias_term = jnp.sum(pair_grad, axis=(0, 1))
-    grad_weight, grad_bias = lax.psum((weight_term, bias_term), ("row", "col"))
+    grad_weight, grad_bias = lax.psum(lax.psum((weight_term, bias_term), "row"), "col")
     return (pair_out, grad_left, grad_right, grad_weight / residues, grad_bias / residues)
 
 

time: 771 us -> 551 us (0.71)
  waiting for transfers between devices: 533 us -> 305 us
    psum x1, waiting for transfers between devices: 230 us -> 62 us  [body(): lax.psum(lax.psum((weight_term, bias_term), 'row'), 'col')]
    all_gather x1, waiting for transfers between devices: 55.6 us -> 0.01 us  [body(): right_all = lax.all_gather(right, 'row', axis=0, tiled=True)]
    psum x1 -> x2, blocking collectives: 77.5 us -> 84.7 us  [the longest x1 65.8 us: body(): lax.psum((weight_term, bias_term), 'row')]
  transfers between devices with their start and end apart: 4 -> 4, of which waited for: 4 -> 3; matrix products, arithmetic and copies ran while one was open for 4% -> 13% of each run, Pallas kernels for 0% -> 0%
where the time goes in v1:
time: 551 us; the launch traced here: 549 us
  waiting for transfers between devices  305 us (55%)
  blocking collectives  114 us (21%)
  matrix products  57.8 us (10%)
  local copies, waits for them, and re-layouts  54.6 us (10%)
  between operations  14.5 us (3%)
    unnamed x6, waiting for transfers between devices  243 us
    psum x1, blocking collectives, body(): lax.psum((weight_term, bias_term), 'row')  65.8 us
    psum x1, waiting for transfers between devices, body(): lax.psum(lax.psum((weight_term, bias_term), 'row'), 'col')  62 us
    all_gather x1, blocking collectives, body(): left_all = lax.all_gather(left, 'col', axis=0, tiled=True)  29.8 us
    psum x1, blocking collectives, body(): lax.psum(lax.psum((weight_term, bias_term), 'row'), 'col')  18.9 us
    dot_general x1, matrix products, body(): jnp.einsum('icje,cez->ijz', outer_split, weight_cube, precision=highest)  17.7 us
    reshape x1, local copies, waits for them, and re-layouts, body(): grad_outer = grad_outer.reshape(tile_rows * C, tile_cols * C)  13.4 us
    dot_general x1, local copies, waits for them, and re-layouts, body(): jnp.einsum('icje,ijz->cez', outer_split, pair_grad, precision=highest)  12.8 us
  transfers between devices with their start and end apart: 4, of which 3 were waited for; matrix products, arithmetic and copies ran while one was open for 13% of the time, Pallas kernels for 0%

profile of v1, /device:TPU:8, one launch (start us, length us, event | category | flops | bytes accessed | tf_op | source)
XLA Modules:
  0.0 549.5 jit_solution(5579469853500991909)
XLA Ops:
  7.2 0.0 copy-start
  7.2 0.0 all-gather.3.cloned.1.call-start
  7.2 0.7 all-gather.3.cloned.1.call-update
  7.9 0.0 all-reduce.7.cloned.1.call-start
  8.0 0.3 copy-done
  8.2 9.8 %convolution_bitcast_fusion = f32[16,32,64,32]{2,3,0,1:T(8,128)} fusion(f32[32,32,128,1]{2,1,3,0:T(8,128)S(1)} %bitcast.43, f32[16,64,128]{2,1,0:T(8,128)} %param.9), kind=kOutput, calls=%fused_computation.1 | convolution fusion | flops 1610612736 | bytes 5242880 | tf_op jit(solution)/shard_map/ijz,cez->icje/dot_general | solution.py:33
  18.0 12.4 %copy.21 = f32[16,32,64,32]{3,2,1,0:T(8,128)} copy(f32[16,32,64,32]{2,3,0,1:T(8,128)} %convolution_bitcast_fusion) | data formatting | bytes 8388608 | tf_op jit(solution)/shard_map/ijz,cez->icje/transpose | solution.py:33
  30.4 0.0 copy-start.3
  30.4 13.4 %reshape.24 = f32[512,2048]{1,0:T(8,128)} reshape(f32[16,32,64,32]{3,2,1,0:T(8,128)} %copy.21) | data formatting | bytes 8388608 | tf_op jit(solution)/shard_map/reshape | solution.py:34
  43.8 0.0 copy-done.3
  43.8 29.8 %all_gather.6 = f32[128,512]{1,0:T(8,128)S(1)} all-gather(f32[16,512]{1,0:T(8,128)S(1)} %copy-done.3), channel_id=1, replica_groups=mesh['row'=32,'col'=8] {'col'}, dimensions={0}, use_global_device_ids=true | all-gather | bytes 294912 | tf_op jit(solution)/shard_map/all_gather | solution.py:19
  73.6 9.9 %fusion = f32[128,2048]{0,1:T(8,128)} fusion(f32[512,2048]{1,0:T(8,128)} %reshape.24, f32[128,512]{1,0:T(8,128)S(1)} %all_gather.6), kind=kOutput, calls=%fused_computation.3 | convolution fusion | flops 1610874880 | bytes 5505024 | tf_op jit(solution)/shard_map/dot_general | solution.py:49
  83.5 0.0 all-gather.3.cloned.1.call-done
  83.5 1.6 reshape.26
  85.1 5.4 convolution_multiply_fusion
  90.4 11.4 %reshape.22 = f32[16,32,64,32]{3,2,1,0:T(8,128)} reshape(f32[512,2048]{1,0:T(8,128)} %convolution_multiply_fusion) | data formatting | bytes 8388608 | tf_op jit(solution)/shard_map/reshape | solution.py:31
  101.9 0.0 copy-start.1
  101.9 12.8 %copy.33 = f32[32,32,16,64]{3,1,0,2:T(8,128)} copy(f32[32,32,16,64]{1,3,0,2:T(8,128)} %bitcast.44) | data formatting | bytes 8388608 | tf_op jit(solution)/shard_map/icje,ijz->cez/dot_general | solution.py:51
  114.7 0.0 copy-start.5
  114.7 0.0 copy-done.1
  114.7 0.0 copy-start.4
  114.7 9.9 %convolution_bitcast_fusion.2 = f32[1024,128]{1,0:T(8,128)} fusion(f32[1024,16,64]{2,0,1:T(8,128)} %bitcast.45, f32[16,64,128]{2,1,0:T(8,128)S(1)} %copy-done.1), kind=kOutput, calls=%fused_computation.5 | convolution fusion | flops 1610612736 | bytes 5242880 | tf_op jit(solution)/shard_map/icje,ijz->cez/dot_general | solution.py:51
  124.6 0.0 all-reduce.7.cloned.1.call-update
  124.6 0.0 all-reduce.5.cloned.1.call-start
  124.7 0.2 reduce_sum.9
  124.8 0.0 copy-done.5
  124.8 0.6 dynamic-slice
  126.0 65.8 %psum.30 = f32[128]{0:T(128)S(1)} all-reduce(f32[128]{0:T(128)S(1)} %reduce_sum.9), channel_id=1, replica_groups=mesh['row'=32,'col'=8] {'row'}, use_global_device_ids=true, to_apply=%region_5.0 | all-reduce | flops 128 | bytes 1024 | tf_op jit(solution)/shard_map/psum | solution.py:55
  191.8 18.9 %psum.31 = f32[128]{0:T(128)S(1)} all-reduce(f32[128]{0:T(128)S(1)} %psum.30), channel_id=1, replica_groups=mesh['row'=32,'col'=8] {'col'}, use_global_device_ids=true, to_apply=%region_6.0 | all-reduce | flops 128 | bytes 1024 | tf_op jit(solution)/shard_map/psum | solution.py:55
  210.7 201.9 %all-reduce.7.cloned.1.call-done = (f32[128,2048]{0,1:T(8,128)}, f32[1024,128]{1,0:T(8,128)}) async-done(((f32[128,2048]{0,1:T(8,128)}, f32[1024,128]{1,0:T(8,128)}), (f32[128,2048]{0,1:T(8,128)}, f32[1024,128]{1,0:T(8,128)})) %all-reduce.7.cloned.1.call-update) | async-done | bytes 1572880
  412.6 0.0 all-reduce.5.cloned.1.call-update
  412.7 0.0 reduce-scatter.5.cloned.1.call-start
  412.7 0.5 broadcast_multiply_fusion.1
  413.2 5.2 fusion.2
  418.4 0.8 copy.29
  419.3 0.0 reduce-scatter.5.cloned.1.call-update
  419.3 0.0 copy-done.4
  419.3 0.0 copy-start.2
  419.3 17.7 %fusion.1 = f32[16,64,128]{2,1,0:T(8,128)} fusion(f32[16,32,64,32]{3,2,1,0:T(8,128)} %reshape.22, f32[32,32,128,1]{2,1,0,3:T(8,128)S(1)} %bitcast.42, f32[128]{0:T(128)S(1)} %copy-done.4), kind=kOutput, calls=%fused_computation.6 | convolution fusion | flops 1610743808 | bytes 5243392 | tf_op jit(solution)/shard_map/icje,cez->ijz/dot_general | solution.py:32
  437.0 0.0 copy-done.2
  437.0 0.3 constant_dynamic-slice_fusion
  437.3 0.9 copy.25
  438.3 62.0 %all-reduce.5.cloned.1.call-done = f32[1024,128]{1,0:T(8,128)} async-done(((f32[1024,128]{1,0:T(8,128)}), f32[1024,128]{1,0:T(8,128)}) %all-reduce.5.cloned.1.call-update) | async-done | bytes 524304 | tf_op jit(solution)/shard_map/psum | solution.py:55
  500.2 1.9 broadcast_multiply_fusion
  502.1 40.9 %reduce-scatter.5.cloned.1.call-done = f32[16,512]{1,0:T(8,128)} async-done(((f32[128,512]{1,0:T(8,128)}), f32[16,512]{1,0:T(8,128)}) %reduce-scatter.5.cloned.1.call-update) | async-done | bytes 32784
Async XLA Ops:
  7.2 1.0 copy-start
  7.2 76.3 %all-gather.3.cloned.1.call-start = ((), (), s32[]{:S(2)}) async-start(), calls=%async_computation.2 | async-start | bytes 1081344 | tf_op jit(solution)/shard_map/all_gather | solution.py:20
  7.9 404.7 %all-reduce.7.cloned.1.call-start = ((), (), s32[]{:S(2)}) async-start(), calls=%async_computation.4 | async-start | bytes 3145728
  30.4 13.4 %copy-start.3 = (f32[16,512]{1,0:T(8,128)S(1)}, f32[16,512]{1,0:T(8,128)}, u32[]{:S(2)}) copy-start(f32[16,512]{1,0:T(8,128)} %param.5) | copy-start | bytes 98308
  101.9 12.8 %copy-start.1 = (f32[16,64,128]{2,1,0:T(8,128)S(1)}, f32[16,64,128]{2,1,0:T(8,128)}, u32[]{:S(2)}) copy-start(f32[16,64,128]{2,1,0:T(8,128)} %param.9) | copy-start | bytes 1572868
  114.7 10.1 %copy-start.5 = (u32[256]{0:T(256)S(1)}, u32[256]{0:T(256)}, u32[]{:S(2)}) copy-start(u32[256]{0:T(256)} %constant.18) | copy-start | bytes 3076
  114.7 304.6 %copy-start.4 = (f32[128]{0:T(128)S(1)}, f32[128]{0:T(128)}, u32[]{:S(2)}) copy-start(f32[128]{0:T(128)} %param.8) | copy-start | bytes 1540
  124.6 375.6 %all-reduce.5.cloned.1.call-start = ((), (), s32[]{:S(2)}) async-start(), calls=%async_computation.1 | async-start | bytes 1048576 | tf_op jit(solution)/shard_map/psum | solution.py:55
  412.7 130.3 %reduce-scatter.5.cloned.1.call-start = ((), (), s32[]{:S(2)}) async-start(), calls=%async_computation.3 | async-start | bytes 294912
  419.3 17.7 %copy-start.2 = (f32[128,2048]{0,1:T(8,128)S(1)}, f32[128,2048]{0,1:T(8,128)}, u32[]{:S(2)}) copy-start(f32[128,2048]{0,1:T(8,128)} %get-tuple-element.20) | copy-start | bytes 3145732
Sparse Core Ops, SparseCore 0:
  10.5 53.8 all-gather.2
  124.7 287.8 all-reduce.6
  415.3 84.9 all-reduce.4
  503.1 39.7 reduce-scatter.4
